TPU v7x, 256 devices: a whole 4x4x8 slice. The times are simulated.
256 devices in a mesh: sta: 32 (over y, z), tpl: 8 (over x, core).
Axes of the slice: x: 4, y: 4, z: 8, core: 2. Of those that a mesh axis runs over, the one named last changes fastest.
Arguments:
- window: bfloat16 [1536, 1024], P('sta', 'tpl'), may hold values from -6 to 6
- prior: bfloat16 [1536, 599], P('sta'), may hold values from -6 to 6
- waves: bfloat16 [256, 128, 600], P('tpl', 'sta'), may hold values from -6 to 6
- chan_list: int32 [256, 128], P('tpl', 'sta'), may hold values from 0 to 1535, as said below
- chan_count: int32 [256], P('tpl'), may hold values from 21 to 120
- station_row: int32 [512], replicated, may hold values from 0 to 511, as said below
Outputs:
- stacked: float32 [256, 1024], P(('tpl', 'sta'))
Inputs may be any that keep to these rules, and one draw needn't show every extreme that they name: station_row is a permutation of 0 to 511; station s's three channels are data rows 3 station_row[s] to 3 station_row[s] + 2, and its station block is station_row[s] // 16. `chan_list`: channel c is component c % 3 of station c // 3. For every group of 32 templates (g * 32 to (g + 1) * 32 - 1) and every aligned run of 4 slots, each station block is named by exactly 4 of those slots, listed or not.
All inputs are finite; a program needn't handle non-finite values.
Results may differ from a plain program's by a relative error of at most 0.0029.
Values may be sent and summed in bfloat16 or wider, within the bound.
A program may use at most 64 MiB of HBM per device.

v0:
```python
import jax
import jax.numpy as jnp
from jax import lax
from jax.sharding import PartitionSpec as P

epsilon = 1e-06


def correlate(data_rows, wave_rows):
    result = lax.conv_general_dilated(
        data_rows[None],
        wave_rows[:, None, :],
        (1,),
        "VALID",
        dimension_numbers=("NCH", "OIH", "NCH"),
        feature_group_count=data_rows.shape[0],
        preferred_element_type=jnp.float32,
    )
    return result[0]


def inverse_energy(rows, lag_count, length):
    squares = rows.astype(jnp.float32) ** 2
    prefix = jnp.concatenate(
        [jnp.zeros((rows.shape[0], 1), jnp.float32), jnp.cumsum(squares, axis=1)], axis=1
    )
    energy = prefix[:, length : length + lag_count] - prefix[:, :lag_count]
    return 1.0 / jnp.sqrt(energy + epsilon)


def unit_waves(waves, listed):
    raw_wave = waves.astype(jnp.float32)
    wave_norms = jnp.sqrt(jnp.sum(raw_wave * raw_wave, axis=-1, keepdims=True) + epsilon)
    return (raw_wave / wave_norms * listed[..., None]).astype(jnp.bfloat16)


def per_device(window, prior, waves, chan_list, chan_count, station_row):
    sta_size = lax.axis_size("sta")
    sta_pos = lax.axis_index("sta")
    whole_time = lax.all_gather(window, "tpl", axis=1, tiled=True)
    extended = jnp.concatenate([prior, whole_time], axis=1)
    block_rows = extended.shape[0]
    lag_count = whole_time.shape[1]
    length = waves.shape[2]
    group_size, slot_count = chan_list.shape
    positions = group_size * slot_count
    capacity = positions // sta_size
    slot_index = sta_pos * slot_count + jnp.arange(slot_count, dtype=jnp.int32)
    listed = (slot_index[None, :] < chan_count[:, None]).astype(jnp.float32)
    normed = unit_waves(waves, listed).reshape(positions, length)
    flat_list = chan_list.reshape(positions)
    data_rows = 3 * jnp.take(station_row, flat_list // 3) + flat_list % 3
    owners = data_rows // block_rows
    local_rows = data_rows % block_rows
    owner_hits = (owners[:, None] == jnp.arange(sta_size, dtype=jnp.int32)[None, :]).astype(
        jnp.int32
    )
    rank_in = jnp.sum(jnp.cumsum(owner_hits, axis=0) * owner_hits, axis=1) - 1
    slot_at = owners * capacity + rank_in
    order_of = (
        jnp.zeros((positions,), jnp.int32).at[slot_at].set(jnp.arange(positions, dtype=jnp.int32))
    )
    template_of = jnp.arange(positions, dtype=jnp.int32) // slot_count
    sent_waves = normed[order_of]
    requests = local_rows[order_of].reshape(sta_size, capacity)
    asked_rows = lax.all_to_all(requests, "sta", split_axis=0, concat_axis=0, tiled=True)
    answer = extended[asked_rows.reshape(positions)].reshape(sta_size, capacity, extended.shape[1])
    received = lax.all_to_all(answer, "sta", split_axis=0, concat_axis=0, tiled=True).reshape(
        positions, extended.shape[1]
    )
    scales = inverse_energy(received, lag_count, length)
    traces = correlate(received, sent_waves) * scales
    buffer_templates = template_of[order_of]
    selector = (
        buffer_templates[None, :] == jnp.arange(group_size, dtype=jnp.int32)[:, None]
    ).astype(jnp.float32)
    return lax.psum_scatter(
        jnp.dot(
            selector, traces, precision=lax.Precision.HIGHEST, preferred_element_type=jnp.float32
        ),
        "sta",
        scatter_dimension=0,
        tiled=True,
    )


def solution(mesh):
    in_specs = (
        P("sta", "tpl"),
        P("sta", None),
        P("tpl", "sta", None),
        P("tpl", "sta"),
        P("tpl"),
        P(),
    )
    out_specs = P(("tpl", "sta"), None)
    return jax.shard_map(
        per_device, mesh=mesh, in_specs=in_specs, out_specs=out_specs, check_vma=False
    )
```

profile of v0, /device:TPU:1, one launch (start us, length us, event | category | flops | bytes accessed | tf_op | source)
XLA Modules:
  0.0 459.0 jit_solution(6063085323114914838)
XLA Ops:
  6.5 0.0 copy-start
  6.5 0.7 sign_compare_fusion
  7.2 0.1 copy.39
  7.3 0.1 ne.135
  7.5 0.0 copy-start.4
  7.5 0.1 ne.129
  7.6 0.6 copy-done.4
  8.2 0.1 copy.41
  8.2 0.1 div.65
  8.4 0.1 div.63
  8.5 0.1 copy.40
  8.5 0.1 rem.72
  8.7 0.1 rem.77
  8.8 0.0 copy-done
  8.8 1.3 gather_fusion
  10.1 0.1 fusion.13
  10.2 0.2 reduce_window_sum.26
  10.4 0.2 select_reduce_fusion
  10.6 1.0 scatter_custom_fusion
  11.6 1.2 gather_fusion.2
  12.8 0.7 all_to_all.9
  13.5 12.2 %all-to-all-start = ((s32[32,1,4]{2,1,0:T(1,128)}), s32[32,1,4]{2,1,0:T(1,128)S(1)}, u32[]{:S(2)}, u32[]{:S(2)}) async-start(s32[32,1,4]{2,1,0:T(1,128)} %bitcast.4), calls=%async_computation | async-start | bytes 32768 | tf_op jit(solution)/shard_map/all_to_all | solution.py:66
  25.7 0.0 copy-start.2
  25.7 0.0 copy-done.3
  25.7 12.7 %all_gather.3 = bf16[48,1024]{1,0:T(8,128)(2,1)S(1)} all-gather(bf16[48,128]{1,0:T(8,128)(2,1)S(1)} %copy-done.3), channel_id=1, replica_groups=mesh['sta'=32,'tpl'=8] {'tpl'}, dimensions={1}, use_global_device_ids=true | all-gather | bytes 110592 | tf_op jit(solution)/shard_map/all_gather | solution.py:40
  38.4 0.0 copy-done.2
  38.4 0.1 pad_maximum_fusion
  38.6 0.0 all-to-all-done
  38.6 0.5 broadcast.386
  39.1 0.7 reduce.3
  39.8 0.1 reshape.271
  39.9 1.0 gather_fusion.3
  40.9 0.9 reshape.272
  41.7 9.6 %all-to-all-start.1 = ((bf16[32,4,1623]{2,1,0:T(4,128)(2,1)}), bf16[32,4,1623]{2,1,0:T(4,128)(2,1)S(1)}, u32[]{:S(2)}, u32[]{:S(2)}) async-start(bf16[32,4,1623]{2,1,0:T(4,128)(2,1)} %reshape.272), calls=%async_computation.1 | async-start | bytes 851968 | tf_op jit(solution)/shard_map/all_to_all | solution.py:68
  51.4 0.0 all-reduce.5.cloned.1.call-start
  51.4 0.0 copy-done.5
  51.4 0.1 compare_convert_fusion
  51.5 0.1 copy.46
  51.6 1.2 gather_fusion.1
  52.8 0.0 copy-done.1
  52.8 0.2 fusion.11
  53.0 0.2 fusion.10
  53.2 0.1 reshape.273
  53.3 0.9 gather_fusion.4
  54.2 0.2 copy.48
  54.4 9.8 %all-to-all-done.1 = bf16[32,4,1623]{2,1,0:T(4,128)(2,1)S(1)} async-done(((bf16[32,4,1623]{2,1,0:T(4,128)(2,1)}), bf16[32,4,1623]{2,1,0:T(4,128)(2,1)S(1)}, u32[]{:S(2)}, u32[]{:S(2)}) %all-to-all-start.1) | async-done | bytes 415520 | tf_op jit(solution)/shard_map/all_to_all | solution.py:68
  64.1 0.2 broadcast_in_dim_reshape.3
  64.3 1.3 copy.47
  65.7 0.1 convert_multiply_fusion
  65.7 0.3 integer_pow.7
  66.0 0.3 copy.52
  66.3 0.1 pad.4.clone
  66.4 0.5 fusion
  66.9 0.1 broadcast_add_fusion
  67.0 0.3 copy.51
  67.3 0.1 slice.34
  67.4 246.1 %fusion.24 = f32[1,128,1024]{1,0,2:T(1,128)S(1)} fusion(bf16[1,128,1623]{1,0,2:T(2,128)(2,1)S(1)} %copy.47, bf16[128,1,600]{0,1,2:T(2,128)(2,1)S(1)} %copy.48), kind=kOutput, calls=%fused_computation.67 | convolution fusion | flops 157286400 | bytes 1093376 | tf_op jit(solution)/shard_map/conv_general_dilated | solution.py:10
  313.4 1.2 fusion.6
  314.6 0.0 all-reduce.5.cloned.1.call-update
  314.6 0.0 copy-start.6
  314.6 0.7 copy-done.6
  315.3 0.6 dynamic-slice
  316.0 134.2 %all-reduce.5.cloned.1.call-done = f32[32,1024]{1,0:T(8,128)} async-done(((f32[32,1024]{1,0:T(8,128)}), f32[32,1024]{1,0:T(8,128)}) %all-reduce.5.cloned.1.call-update) | async-done | bytes 131088
  450.2 2.0 constant_dynamic-slice_fusion
  (19 shorter events, 0.2 us)
Async XLA Ops:
  6.5 2.3 copy-start
  7.5 0.7 copy-start.4
  13.5 12.2 %copy-start.3 = (bf16[48,128]{1,0:T(8,128)(2,1)S(1)}, bf16[48,128]{1,0:T(8,128)(2,1)}, u32[]{:S(2)}) copy-start(bf16[48,128]{1,0:T(8,128)(2,1)} %param.6) | copy-start | bytes 36868
  13.5 25.0 %all-to-all-start = ((s32[32,1,4]{2,1,0:T(1,128)}), s32[32,1,4]{2,1,0:T(1,128)S(1)}, u32[]{:S(2)}, u32[]{:S(2)}) async-start(s32[32,1,4]{2,1,0:T(1,128)} %bitcast.4), calls=%async_computation | async-start | bytes 32768 | tf_op jit(solution)/shard_map/all_to_all | solution.py:66
  25.7 12.7 %copy-start.2 = (bf16[48,599]{1,0:T(8,128)(2,1)S(1)}, bf16[48,599]{1,0:T(8,128)(2,1)}, u32[]{:S(2)}) copy-start(bf16[48,599]{1,0:T(8,128)(2,1)} %param.7) | copy-start | bytes 172516
  41.7 9.7 %copy-start.5 = (s32[32]{0:T(128)S(1)}, s32[32]{0:T(128)}, u32[]{:S(2)}) copy-start(s32[32]{0:T(128)} %param.10) | copy-start | bytes 388
  41.7 22.4 %all-to-all-start.1 = ((bf16[32,4,1623]{2,1,0:T(4,128)(2,1)}), bf16[32,4,1623]{2,1,0:T(4,128)(2,1)S(1)}, u32[]{:S(2)}, u32[]{:S(2)}) async-start(bf16[32,4,1623]{2,1,0:T(4,128)(2,1)} %reshape.272), calls=%async_computation.1 | async-start | bytes 851968 | tf_op jit(solution)/shard_map/all_to_all | solution.py:68
  51.4 398.8 %all-reduce.5.cloned.1.call-start = ((), (), s32[]{:S(2)}) async-start(), calls=%async_computation.2 | async-start | bytes 262144
  51.6 1.2 copy-start.1
  314.6 0.7 copy-start.6
Sparse Core Ops, SparseCore 0:
  314.8 135.3 all-reduce.4
where the time goes:
time: 462 us; the launch traced here: 459 us
  matrix products  247 us (53%)
  waiting for transfers between devices  144 us (31%)
  starting transfers between devices  21.8 us (5%)
  local copies, waits for them, and re-layouts  16.4 us (4%)
  between operations  13.8 us (3%)
  blocking collectives  12.7 us (3%)
    conv_general_dilated x1, matrix products, correlate(): lax.conv_general_dilated(data_rows[None], wave_rows[:, None, :], (1,), 'V...  246 us
    unnamed x2, waiting for transfers between devices  134 us
    all_gather x1, blocking collectives, per_device(): whole_time = lax.all_gather(window, 'tpl', axis=1, tiled=True)  12.7 us
    all_to_all x1, starting transfers between devices, per_device(): lax.all_to_all(requests, 'sta', split_axis=0, concat_axis=0, tiled=True)  12.2 us
    all_to_all x1, waiting for transfers between devices, per_device(): lax.all_to_all(answer, 'sta', split_axis=0, concat_axis=0, tiled=True)  9.76 us
    all_to_all x1, starting transfers between devices, per_device(): lax.all_to_all(answer, 'sta', split_axis=0, concat_axis=0, tiled=True)  9.63 us
  transfers between devices with their start and end apart: 3, of which 2 were waited for; matrix products, arithmetic and copies ran while one was open for 1% of the time, Pallas kernels for 0%

commit v1 on v0

v1 whole, which is shorter than its diff:
```python
import functools

import jax
import jax.numpy as jnp
from jax import lax
from jax.experimental import pallas as pl
from jax.experimental.pallas import tpu as pltpu
from jax.sharding import PartitionSpec as P

EPSILON = 1e-06
MESH = pl.DeviceIdType.MESH
F32 = jnp.float32
BF16 = jnp.bfloat16
I32 = jnp.int32
NT = (((1,), (1,)), ((), ()))
NN = (((1,), (0,)), ((), ()))

LANES = 128
SUB = 32
QUARTERS = LANES // SUB


def iota(shape, dim):
    return lax.broadcasted_iota(I32, shape, dim)


def dot(a, b, dims):
    return lax.dot_general(a, b, dims, preferred_element_type=F32)


def shift_left(v, n):
    width = v.shape[1]
    return v if n == 0 else pltpu.roll(v, width - n, 1)


def kernel(
    cfg,
    window_ref,
    prior_ref,
    waves_ref,
    chan_ref,
    count_ref,
    table_ref,
    out_ref,
    win,
    flat,
    sbuf,
    rbuf,
    mrow,
    mbuf,
    msm,
    xs,
    xall,
    sc,
    ohl,
    obuf,
    rres,
    win_send,
    win_recv,
    wave_send,
    wave_recv,
    meta_send,
    meta_recv,
    res_send,
    res_recv,
    sm_sem,
):
    n_sta, n_tpl, group, slots, length, rows, lags = cfg
    positions = group * slots
    prior_len = length - 1
    cells = lags // LANES
    k_blocks = pl.cdiv(length + SUB - 1, LANES)
    k_width = k_blocks * LANES
    x_blocks = pl.cdiv(prior_len + lags, LANES)
    pitch = 16
    me = lax.axis_index("sta")
    my_t = lax.axis_index("tpl")

    barrier = pltpu.get_barrier_semaphore()

    def greet_sta(o, _):
        pl.semaphore_signal(
            barrier, inc=1, device_id={"sta": lax.rem(me + o, n_sta)}, device_id_type=MESH
        )
        return 0

    def greet_tpl(o, _):
        pl.semaphore_signal(
            barrier, inc=1, device_id={"tpl": lax.rem(my_t + o, n_tpl)}, device_id_type=MESH
        )
        return 0

    lax.fori_loop(1, n_tpl, greet_tpl, 0)
    lax.fori_loop(1, n_sta, greet_sta, 0)

    square = (positions, positions)
    lane = iota(square, 1)
    sub = iota(square, 0)
    lane1 = iota((1, positions), 1)
    template = lane1 % group

    def to_rows(row):
        return jnp.broadcast_to(row, square).T

    chan = jnp.concatenate([chan_ref[j : j + 1, :] for j in range(slots)], axis=1)
    counts = jnp.concatenate([count_ref[...]] * slots, axis=1)
    station = (chan * 43691) >> 17
    station_rows = to_rows(station)
    looked = jnp.zeros(square, I32)
    for h in range(table_ref.shape[1] // LANES):
        entries = jnp.broadcast_to(table_ref[:, pl.ds(LANES * h, LANES)], square)
        looked = jnp.where(station_rows == lane + LANES * h, entries, looked)
    looked = jnp.sum(looked.T, axis=0, keepdims=True)
    block_stations = rows // 3
    owner = looked // block_stations
    local = 3 * (looked % block_stations) + chan - 3 * station
    cap = positions // n_sta
    before = (to_rows(owner) == owner) & (sub < lane)
    rank = jnp.sum(jnp.where(before, 1, 0), axis=0, keepdims=True)
    slot_at = owner * cap + rank
    place = sub == slot_at
    listed = jnp.where(me * slots + lane1 // group < counts, 1.0, 0.0)
    code_rows = to_rows(local * group + template)
    mrow[...] = jnp.sum(jnp.where(to_rows(slot_at) == lane, code_rows, 0), axis=0, keepdims=True)

    for t in range(0, group):
        wave = waves_ref[t].astype(F32)
        wave = jnp.concatenate([wave, jnp.zeros((slots, k_width - length), F32)], axis=1)
        for r in range(k_blocks):
            flat[r, pl.ds(t, slots, stride=group), :] = wave[:, LANES * r : LANES * (r + 1)]
    mover = jnp.where(place, jnp.broadcast_to(listed, (positions, positions)), 0.0).astype(BF16)
    moved = jnp.concatenate(
        [dot(mover, flat[r].astype(BF16), NN) for r in range(k_blocks)], axis=1
    )
    norms = jnp.sqrt(jnp.sum(moved * moved, axis=1, keepdims=True) + EPSILON)
    normed = moved / norms
    for s in range(n_sta):
        sbuf[s] = normed[cap * s : cap * (s + 1)].astype(BF16)

    pl.semaphore_wait(barrier, n_sta + n_tpl - 2)

    def win_copy(slot, peer):
        return pltpu.make_async_remote_copy(
            src_ref=window_ref,
            dst_ref=win.at[slot],
            send_sem=win_send.at[peer],
            recv_sem=win_recv.at[slot],
            device_id={"tpl": peer},
            device_id_type=MESH,
        )

    def wave_copy(slot, peer):
        return pltpu.make_async_remote_copy(
            src_ref=sbuf.at[peer],
            dst_ref=rbuf.at[slot],
            send_sem=wave_send.at[peer],
            recv_sem=wave_recv.at[slot],
            device_id={"sta": peer},
            device_id_type=MESH,
        )

    def meta_copy(slot, peer):
        return pltpu.make_async_remote_copy(
            src_ref=mrow,
            dst_ref=mbuf.at[slot],
            send_sem=meta_send.at[peer],
            recv_sem=meta_recv.at[slot],
            device_id={"sta": peer},
            device_id_type=MESH,
        )

    def res_copy(slot, peer):
        return pltpu.make_async_remote_copy(
            src_ref=obuf.at[peer],
            dst_ref=rres.at[slot],
            send_sem=res_send.at[peer],
            recv_sem=res_recv.at[slot],
            device_id={"sta": peer},
            device_id_type=MESH,
        )

    def over(count, first, body):
        def step(o, _):
            body(lax.rem(first + o, count))
            return 0

        lax.fori_loop(1, count, step, 0)

    over(n_tpl, my_t, lambda peer: win_copy(my_t, peer).start())

    def send_waves(peer):
        meta_copy(me, peer).start()
        wave_copy(me, peer).start()

    over(n_sta, me, send_waves)
    win[my_t] = window_ref[...]
    rbuf[me] = sbuf[me]
    mbuf[me] = mrow[...]

    over(n_tpl, my_t, lambda peer: win_copy(peer, peer).wait_recv())

    lane_p = iota((8, LANES), 1)
    prior_tiles = prior_len // LANES
    prior_rest = prior_len % LANES

    for g in range(rows // 8):
        r8 = pl.ds(8 * g, 8)
        old = prior_ref[r8, :].astype(F32)
        new = jnp.concatenate(
            [win[p, r8, :].astype(F32) for p in range(n_tpl)] + [jnp.zeros((8, LANES), F32)], axis=1
        )
        new = pltpu.roll(new, prior_rest, 1)
        tail = jnp.concatenate(
            [old[:, prior_tiles * LANES :], jnp.zeros((8, LANES - prior_rest), F32)], axis=1
        )
        joint = jnp.where(lane_p < prior_rest, tail, new[:, :LANES])
        x = jnp.concatenate([old[:, : prior_tiles * LANES], joint, new[:, LANES:]], axis=1)
        for b in range(QUARTERS):
            moved_x = shift_left(x, SUB * b)
            for m in range(x_blocks):
                xs[b, pl.ds(pitch * 8 * g + m, 8, stride=pitch), :] = moved_x[
                    :, LANES * m : LANES * (m + 1)
                ]
        sums = {1: x * x}
        size = 1
        while 2 * size <= length:
            sums[2 * size] = sums[size] + shift_left(sums[size], size)
            size *= 2
        energy, done = None, 0
        while size:
            if length & size:
                part = shift_left(sums[size], done)
                energy = part if energy is None else energy + part
                done += size
            size //= 2
        scale = 1.0 / jnp.sqrt(energy[:, :lags] + EPSILON)
        for a in range(cells):
            sc[r8, a, :] = scale[:, LANES * a : LANES * (a + 1)]

    def build_row(c, _):
        for r in range(k_blocks):
            for b in range(0, QUARTERS, 2):
                pair = jnp.concatenate(
                    [xs[b + d, pl.ds(pitch * c + r, cells), :] for d in range(2)], axis=0
                )
                xall[c, pl.ds(cells * b, 2 * cells), pl.ds(LANES * r, LANES)] = pair.astype(BF16)
        return 0

    lax.fori_loop(0, rows, build_row, 0)

    def take(peer):
        meta_copy(peer, peer).wait_recv()
        wave_copy(peer, peer).wait_recv()

    over(n_sta, me, take)
    to_sm = pltpu.make_async_copy(mbuf, msm, sm_sem)
    to_sm.start()
    to_sm.wait()

    quarter = iota((8, LANES), 1) // SUB

    def pick(parts):
        value = parts[0]
        for i in range(1, QUARTERS):
            value = jnp.where(quarter == i, parts[i], value)
        return value

    def correlate(s, _):
        wave = rbuf[s].astype(F32)
        codes = [msm[s, 0, cap * me + i] for i in range(cap)]
        local_rows = [code >> (group.bit_length() - 1) for code in codes]
        shifted = jnp.concatenate(
            [
                pltpu.roll(
                    jnp.broadcast_to(wave[i : i + 1], (SUB, k_width)), 0, 1, stride=1, stride_axis=0
                )
                for i in range(cap)
            ],
            axis=0,
        ).astype(BF16)
        data = jnp.concatenate([xall[c] for c in local_rows], axis=0)
        found = dot(data, shifted, NT)
        block = lambda i, b: found[SUB * i + cells * b : SUB * i + cells * (b + 1)]
        turned = []
        for d in range(QUARTERS):
            v = pick([block(i, (i + d) % QUARTERS) for i in range(cap)])
            turned.append(v if d == 0 else pltpu.roll(v, SUB * d, 1))
        out = []
        for i in range(cap):
            v = pick([turned[(b - i) % QUARTERS] for b in range(QUARTERS)])
            out.append(v * sc[local_rows[i]])
        traces = jnp.concatenate(out, axis=0)
        hi = traces.astype(BF16)
        lo = (traces - hi.astype(F32)).astype(BF16)
        here = pl.ds(pl.multiple_of(cells * cap * s, cells * cap), cells * cap)
        ohl[here, pl.ds(0, LANES)] = hi
        ohl[here, pl.ds(LANES, LANES)] = lo
        return 0

    lax.fori_loop(0, n_sta, correlate, 0)

    codes = mbuf[...].reshape(n_sta, LANES)
    mine = pltpu.roll(codes, lax.rem(positions - cap * me, positions), 1)
    tmpl = mine & (group - 1)
    lane_s = iota((n_sta, LANES), 1)
    sub_s = iota((n_sta, LANES), 0)
    by_lane = jnp.zeros((n_sta, LANES), I32)
    for j in range(cap):
        by_lane = jnp.where(
            (lane_s // cells) % cap == j, jnp.broadcast_to(tmpl[:, j : j + 1], (n_sta, LANES)), by_lane
        )
    per_tile = LANES // (cap * cells)
    by_lane = by_lane.astype(F32)
    out_rows = group * cells
    row_t = (iota((out_rows, LANES), 0) // cells).astype(F32)
    same_a = iota((out_rows, LANES), 0) % cells == iota((out_rows, LANES), 1) % cells
    tiles = []
    for m in range(positions * cells // LANES):
        names = jnp.sum(
            jnp.where(sub_s == per_tile * m + lane_s // (cap * cells), by_lane, 0.0),
            axis=0,
            keepdims=True,
        )
        tiles.append(jnp.where((row_t == names) & same_a, 1.0, 0.0).astype(BF16))
    chooser = jnp.concatenate(tiles, axis=1)
    both = dot(chooser, ohl[...], NN)
    stacked = both[:, :LANES] + both[:, LANES:]
    for t in range(group):
        obuf[t] = stacked[cells * t : cells * (t + 1)]

    over(n_sta, me, lambda peer: res_copy(me, peer).start())
    rres[me] = obuf[me]
    over(n_sta, me, lambda peer: res_copy(peer, peer).wait_recv())
    total = jnp.sum(rres[...], axis=0)
    for a in range(cells):
        out_ref[0:1, pl.ds(LANES * a, LANES)] = total[a : a + 1]

    over(n_tpl, my_t, lambda peer: win_copy(my_t, peer).wait_send())

    def drain(peer):
        meta_copy(me, peer).wait_send()
        wave_copy(me, peer).wait_send()
        res_copy(me, peer).wait_send()

    over(n_sta, me, drain)


def solution(mesh):
    n_sta, n_tpl = mesh.shape["sta"], mesh.shape["tpl"]

    def per_device(window, prior, waves, chan_list, chan_count, station_row):
        group, slots, length = waves.shape
        rows = window.shape[0]
        lags = window.shape[1] * n_tpl
        positions = group * slots
        cap = positions // n_sta
        cells = lags // LANES
        k_width = pl.cdiv(length + SUB - 1, LANES) * LANES
        cfg = (n_sta, n_tpl, group, slots, length, rows, lags)
        vmem = pl.BlockSpec(memory_space=pltpu.VMEM)
        dma = pltpu.SemaphoreType.DMA
        return pl.pallas_call(
            functools.partial(kernel, cfg),
            out_shape=jax.ShapeDtypeStruct((1, lags), F32),
            in_specs=[vmem] * 6,
            out_specs=vmem,
            scratch_shapes=[
                pltpu.VMEM((n_tpl, rows, window.shape[1]), BF16),
                pltpu.VMEM((k_width // LANES, positions, LANES), F32),
                pltpu.VMEM((n_sta, cap, k_width), BF16),
                pltpu.VMEM((n_sta, cap, k_width), BF16),
                pltpu.VMEM((1, positions), I32),
                pltpu.VMEM((n_sta, 1, positions), I32),
                pltpu.SMEM((n_sta, 1, positions), I32),
                pltpu.VMEM((QUARTERS, rows * 16, LANES), F32),
                pltpu.VMEM((rows, SUB, k_width), BF16),
                pltpu.VMEM((rows, cells, LANES), F32),
                pltpu.VMEM((positions * cells, 2 * LANES), BF16),
                pltpu.VMEM((group, cells, LANES), F32),
                pltpu.VMEM((n_sta, cells, LANES), F32),
                dma((n_tpl,)),
                dma((n_tpl,)),
                dma((n_sta,)),
                dma((n_sta,)),
                dma((n_sta,)),
                dma((n_sta,)),
                dma((n_sta,)),
                dma((n_sta,)),
                dma(()),
            ],
            compiler_params=pltpu.CompilerParams(collective_id=0, has_side_effects=True),
        )(
            window,
            prior,
            waves,
            chan_list.T,
            chan_count.reshape(1, group),
            station_row.reshape(1, -1),
        )

    return jax.shard_map(
        per_device,
        mesh=mesh,
        in_specs=(
            P("sta", "tpl"),
            P("sta", None),
            P("tpl", "sta", None),
            P("tpl", "sta"),
            P("tpl"),
            P(),
        ),
        out_specs=P(("tpl", "sta"), None),
        check_vma=False,
    )
```

time: 462 us -> 43 us (0.09)
  matrix products: 247 us -> 0 us
  waiting for transfers between devices: 144 us -> 0 us
  Pallas kernels: 0 us -> 41.6 us
  starting transfers between devices: 21.8 us -> 0 us
  local copies, waits for them, and re-layouts: 16.4 us -> 1.28 us
  between operations: 13.8 us -> 0.01 us
  blocking collectives: 12.7 us -> 0 us
    conv_general_dilated x1 -> x0, matrix products: 246 us -> none  [correlate(): lax.conv_general_dilated(data_rows[None], wave_rows[:, None, :], (1,), 'V...]
    unnamed x2 -> x0, waiting for transfers between devices: 134 us -> none
    pallas_call x0 -> x1, Pallas kernels: none -> 41.6 us  [per_device(): pl.pallas_call(functools.partial(kernel, cfg), out_shape=jax.ShapeDtypeSt...]
    all_to_all x2 -> x0, starting transfers between devices: 21.8 us -> none  [the longest x1 12.2 us: per_device(): lax.all_to_all(requests, 'sta', split_axis=0, concat_axis=0, tiled=True)]
    all_gather x1 -> x0, blocking collectives: 12.7 us -> none  [per_device(): whole_time = lax.all_gather(window, 'tpl', axis=1, tiled=True)]
    all_to_all x2 -> x0, waiting for transfers between devices: 9.76 us -> none  [the longest x1 9.76 us: per_device(): lax.all_to_all(answer, 'sta', split_axis=0, concat_axis=0, tiled=True)]
    gather x5 -> x0, local copies, waits for them, and re-layouts: 5.56 us -> none  [the longest x1 1.27 us: per_device(): data_rows = 3 * jnp.take(station_row, flat_list // 3) + flat_list % 3]
  transfers between devices with their start and end apart: 3 -> 0, of which waited for: 2 -> 0; matrix products, arithmetic and copies ran while one was open for 1% -> 0% of each run, Pallas kernels for 0% -> 0%
where the time goes in v1:
time: 43 us; the launch traced here: 42.8 us
  Pallas kernels  41.6 us (97%)
  local copies, waits for them, and re-layouts  1.28 us (3%)
    pallas_call x1, Pallas kernels, per_device(): pl.pallas_call(functools.partial(kernel, cfg), out_shape=jax.ShapeDtypeSt...  41.6 us
    unnamed x1, local copies, waits for them, and re-layouts  1.28 us

profile of v1, /device:TPU:1, one launch (start us, length us, event | category | flops | bytes accessed | tf_op | source)
XLA Modules:
  0.0 42.8 jit_solution(13783839194568205418)
XLA Ops:
  0.0 41.6 %shard_map.64 = f32[1,1024]{1,0:T(1,128)} custom-call(bf16[48,128]{1,0:T(8,128)(2,1)} %window_ref.1, bf16[48,599]{1,0:T(8,128)(2,1)} %prior_ref.1, bf16[32,4,600]{2,1,0:T(4,128)(2,1)} %waves_ref.1, s32[4,32]{1,0:T(4,128)} %bitcast.3, s32[1,32]{1,0:T(1,128)} %bitcast.5, s32[1,512]{1,0:T(1,128)} %bitcast.4), custom_call_target="tpu_custom_call" | custom-call | tf_op jit(solution)/shard_map/pallas_call | solution.py:362
  41.6 1.3 %copy.8 = f32[1,1024]{1,0:T(1,128)} copy(f32[1,1024]{1,0:T(1,128)} %shard_map.64) | data formatting | bytes 8192

commit v2 on v1

--- a/solution.py
+++ b/solution.py
@@ -17,6 +17,7 @@
 
 LANES = 128
 SUB = 32
+BATCH = 8
 QUARTERS = LANES // SUB
 
 
@@ -35,13 +36,19 @@
 
 def kernel(
     cfg,
+    window_hbm,
+    prior_hbm,
+    waves_hbm,
+    chan_hbm,
+    count_hbm,
+    table_hbm,
+    out_ref,
     window_ref,
     prior_ref,
     waves_ref,
     chan_ref,
     count_ref,
     table_ref,
-    out_ref,
     win,
     flat,
     sbuf,
@@ -64,24 +71,32 @@
     res_send,
     res_recv,
     sm_sem,
+    in_sem,
 ):
-    n_sta, n_tpl, group, slots, length, rows, lags = cfg
+    n_sta, n_tpl, group, slots, length, rows, lags, z_size = cfg
     positions = group * slots
     prior_len = length - 1
     cells = lags // LANES
     k_blocks = pl.cdiv(length + SUB - 1, LANES)
     k_width = k_blocks * LANES
     x_blocks = pl.cdiv(prior_len + lags, LANES)
-    pitch = 16
+    pitch = x_blocks
     me = lax.axis_index("sta")
     my_t = lax.axis_index("tpl")
 
+    my_y, my_z = me // z_size, me % z_size
+    y_size = n_sta // z_size
+
+    def peer_of(k):
+        i, j = k // y_size, k % y_size
+        dz = z_size // 2 + jnp.where(i % 2 == 1, -((i + 1) // 2), i // 2)
+        dy = y_size // 2 + jnp.where(j % 2 == 1, -((j + 1) // 2), j // 2)
+        return ((my_y + dy) % y_size) * z_size + (my_z + dz) % z_size
+
     barrier = pltpu.get_barrier_semaphore()
 
-    def greet_sta(o, _):
-        pl.semaphore_signal(
-            barrier, inc=1, device_id={"sta": lax.rem(me + o, n_sta)}, device_id_type=MESH
-        )
+    def greet_sta(k, _):
+        pl.semaphore_signal(barrier, inc=1, device_id={"sta": peer_of(k)}, device_id_type=MESH)
         return 0
 
     def greet_tpl(o, _):
@@ -90,8 +105,25 @@
         )
         return 0
 
+    inputs = [
+        pltpu.make_async_copy(src, dst, in_sem.at[n])
+        for n, (src, dst) in enumerate(
+            [
+                (chan_hbm, chan_ref),
+                (count_hbm, count_ref),
+                (table_hbm, table_ref),
+                (waves_hbm, waves_ref),
+                (window_hbm, window_ref),
+                (prior_hbm, prior_ref),
+            ]
+        )
+    ]
+    for copy in inputs:
+        copy.start()
+    lax.fori_loop(0, n_sta - 1, greet_sta, 0)
     lax.fori_loop(1, n_tpl, greet_tpl, 0)
-    lax.fori_loop(1, n_sta, greet_sta, 0)
+    for copy in inputs:
+        copy.wait()
 
     square = (positions, positions)
     lane = iota(square, 1)
@@ -139,65 +171,59 @@
 
     pl.semaphore_wait(barrier, n_sta + n_tpl - 2)
 
+    def remote(src, dst, send, recv, device):
+        return pltpu.make_async_remote_copy(
+            src_ref=src,
+            dst_ref=dst,
+            send_sem=send,
+            recv_sem=recv,
+            device_id=device,
+            device_id_type=MESH,
+        )
+
     def win_copy(slot, peer):
-        return pltpu.make_async_remote_copy(
-            src_ref=window_ref,
-            dst_ref=win.at[slot],
-            send_sem=win_send.at[peer],
-            recv_sem=win_recv.at[slot],
-            device_id={"tpl": peer},
-            device_id_type=MESH,
-        )
-
-    def wave_copy(slot, peer):
-        return pltpu.make_async_remote_copy(
-            src_ref=sbuf.at[peer],
-            dst_ref=rbuf.at[slot],
-            send_sem=wave_send.at[peer],
-            recv_sem=wave_recv.at[slot],
-            device_id={"sta": peer},
-            device_id_type=MESH,
-        )
-
-    def meta_copy(slot, peer):
-        return pltpu.make_async_remote_copy(
-            src_ref=mrow,
-            dst_ref=mbuf.at[slot],
-            send_sem=meta_send.at[peer],
-            recv_sem=meta_recv.at[slot],
-            device_id={"sta": peer},
-            device_id_type=MESH,
-        )
-
-    def res_copy(slot, peer):
-        return pltpu.make_async_remote_copy(
-            src_ref=obuf.at[peer],
-            dst_ref=rres.at[slot],
-            send_sem=res_send.at[peer],
-            recv_sem=res_recv.at[slot],
-            device_id={"sta": peer},
-            device_id_type=MESH,
-        )
-
-    def over(count, first, body):
+        return remote(window_ref, win.at[slot], win_send.at[peer], win_recv.at[slot], {"tpl": peer})
+
+    def wave_copy(k, peer):
+        return remote(
+            sbuf.at[peer], rbuf.at[k], wave_send, wave_recv.at[k // BATCH], {"sta": peer}
+        )
+
+    def meta_copy(k, peer):
+        return remote(
+            mrow, mbuf.at[k], meta_send, meta_recv.at[k // BATCH], {"sta": peer}
+        )
+
+    def res_copy(k, peer):
+        return remote(obuf.at[peer], rres.at[k], res_send, res_recv, {"sta": peer})
+
+    def over_tpl(body):
         def step(o, _):
-            body(lax.rem(first + o, count))
+            body(lax.rem(my_t + o, n_tpl))
             return 0
 
-        lax.fori_loop(1, count, step, 0)
-
-    over(n_tpl, my_t, lambda peer: win_copy(my_t, peer).start())
-
-    def send_waves(peer):
-        meta_copy(me, peer).start()
-        wave_copy(me, peer).start()
-
-    over(n_sta, me, send_waves)
+        lax.fori_loop(1, n_tpl, step, 0)
+
+    def over_sta(body):
+        def step(k, _):
+            body(k, peer_of(k))
+            return 0
+
+        lax.fori_loop(0, n_sta - 1, step, 0)
+
+    batches = n_sta // BATCH
+
+    def batch_of(g):
+        return pl.ds(BATCH * g, BATCH - 1 if g == batches - 1 else BATCH)
+
+    over_sta(lambda k, peer: meta_copy(k, peer).start())
+    over_tpl(lambda peer: win_copy(my_t, peer).start())
+    over_sta(lambda k, peer: wave_copy(k, peer).start())
     win[my_t] = window_ref[...]
-    rbuf[me] = sbuf[me]
-    mbuf[me] = mrow[...]
-
-    over(n_tpl, my_t, lambda peer: win_copy(peer, peer).wait_recv())
+    rbuf[n_sta - 1] = sbuf[me]
+    mbuf[n_sta - 1] = mrow[...]
+
+    over_tpl(lambda peer: win_copy(peer, peer).wait_recv())
 
     lane_p = iota((8, LANES), 1)
     prior_tiles = prior_len // LANES
@@ -246,16 +272,7 @@
                 xall[c, pl.ds(cells * b, 2 * cells), pl.ds(LANES * r, LANES)] = pair.astype(BF16)
         return 0
 
-    lax.fori_loop(0, rows, build_row, 0)
-
-    def take(peer):
-        meta_copy(peer, peer).wait_recv()
-        wave_copy(peer, peer).wait_recv()
-
-    over(n_sta, me, take)
-    to_sm = pltpu.make_async_copy(mbuf, msm, sm_sem)
-    to_sm.start()
-    to_sm.wait()
+    lax.fori_loop(0, rows, build_row, 0, unroll=4)
 
     quarter = iota((8, LANES), 1) // SUB
 
@@ -265,7 +282,7 @@
             value = jnp.where(quarter == i, parts[i], value)
         return value
 
-    def correlate(s, _):
+    def correlate(s):
         wave = rbuf[s].astype(F32)
         codes = [msm[s, 0, cap * me + i] for i in range(cap)]
         local_rows = [code >> (group.bit_length() - 1) for code in codes]
@@ -292,12 +309,31 @@
         traces = jnp.concatenate(out, axis=0)
         hi = traces.astype(BF16)
         lo = (traces - hi.astype(F32)).astype(BF16)
-        here = pl.ds(pl.multiple_of(cells * cap * s, cells * cap), cells * cap)
+        here = pl.ds(cells * cap * s, cells * cap)
         ohl[here, pl.ds(0, LANES)] = hi
         ohl[here, pl.ds(LANES, LANES)] = lo
-        return 0
-
-    lax.fori_loop(0, n_sta, correlate, 0)
+
+    def to_scalars(g):
+        here = pl.ds(BATCH * g, BATCH)
+        return pltpu.make_async_copy(mbuf.at[here], msm.at[here], sm_sem.at[g])
+
+    def meta_here(g):
+        here = batch_of(g)
+        remote(mbuf.at[here], mbuf.at[here], meta_send, meta_recv.at[g], {"sta": me}).wait_recv()
+        to_scalars(g).start()
+
+    def waves_here(g):
+        here = batch_of(g)
+        remote(rbuf.at[here], rbuf.at[here], wave_send, wave_recv.at[g], {"sta": me}).wait_recv()
+
+    meta_here(batches - 1)
+    for g in reversed(range(batches)):
+        if g:
+            meta_here(g - 1)
+        waves_here(g)
+        to_scalars(g).wait()
+        for k in range(BATCH):
+            correlate(BATCH * g + k)
 
     codes = mbuf[...].reshape(n_sta, LANES)
     mine = pltpu.roll(codes, lax.rem(positions - cap * me, positions), 1)
@@ -328,21 +364,18 @@
     for t in range(group):
         obuf[t] = stacked[cells * t : cells * (t + 1)]
 
-    over(n_sta, me, lambda peer: res_copy(me, peer).start())
-    rres[me] = obuf[me]
-    over(n_sta, me, lambda peer: res_copy(peer, peer).wait_recv())
+    over_sta(lambda k, peer: res_copy(k, peer).start())
+    rres[n_sta - 1] = obuf[me]
+    others = pl.ds(0, n_sta - 1)
+    over_tpl(lambda peer: win_copy(my_t, peer).wait_send())
+    remote(mbuf.at[others], mbuf.at[others], meta_send, meta_recv.at[0], {"sta": me}).wait_send()
+    remote(sbuf.at[others], sbuf.at[others], wave_send, wave_recv.at[0], {"sta": me}).wait_send()
+    results = remote(obuf.at[others], rres.at[others], res_send, res_recv, {"sta": me})
+    results.wait_send()
+    results.wait_recv()
     total = jnp.sum(rres[...], axis=0)
     for a in range(cells):
         out_ref[0:1, pl.ds(LANES * a, LANES)] = total[a : a + 1]
-
-    over(n_tpl, my_t, lambda peer: win_copy(my_t, peer).wait_send())
-
-    def drain(peer):
-        meta_copy(me, peer).wait_send()
-        wave_copy(me, peer).wait_send()
-        res_copy(me, peer).wait_send()
-
-    over(n_sta, me, drain)
 
 
 def solution(mesh):
@@ -356,15 +389,21 @@
         cap = positions // n_sta
         cells = lags // LANES
         k_width = pl.cdiv(length + SUB - 1, LANES) * LANES
-        cfg = (n_sta, n_tpl, group, slots, length, rows, lags)
+        cfg = (n_sta, n_tpl, group, slots, length, rows, lags, 8)
         vmem = pl.BlockSpec(memory_space=pltpu.VMEM)
         dma = pltpu.SemaphoreType.DMA
         return pl.pallas_call(
             functools.partial(kernel, cfg),
             out_shape=jax.ShapeDtypeStruct((1, lags), F32),
-            in_specs=[vmem] * 6,
+            in_specs=[pl.BlockSpec(memory_space=pl.ANY)] * 6,
             out_specs=vmem,
             scratch_shapes=[
+                pltpu.VMEM(window.shape, BF16),
+                pltpu.VMEM(prior.shape, BF16),
+                pltpu.VMEM(waves.shape, BF16),
+                pltpu.VMEM((slots, group), I32),
+                pltpu.VMEM((1, group), I32),
+                pltpu.VMEM((1, station_row.shape[0]), I32),
                 pltpu.VMEM((n_tpl, rows, window.shape[1]), BF16),
                 pltpu.VMEM((k_width // LANES, positions, LANES), F32),
                 pltpu.VMEM((n_sta, cap, k_width), BF16),
@@ -372,7 +411,7 @@
                 pltpu.VMEM((1, positions), I32),
                 pltpu.VMEM((n_sta, 1, positions), I32),
                 pltpu.SMEM((n_sta, 1, positions), I32),
-                pltpu.VMEM((QUARTERS, rows * 16, LANES), F32),
+                pltpu.VMEM((QUARTERS, rows * pl.cdiv(length - 1 + lags, LANES), LANES), F32),
                 pltpu.VMEM((rows, SUB, k_width), BF16),
                 pltpu.VMEM((rows, cells, LANES), F32),
                 pltpu.VMEM((positions * cells, 2 * LANES), BF16),
@@ -380,13 +419,14 @@
                 pltpu.VMEM((n_sta, cells, LANES), F32),
                 dma((n_tpl,)),
                 dma((n_tpl,)),
-                dma((n_sta,)),
-                dma((n_sta,)),
-                dma((n_sta,)),
-                dma((n_sta,)),
-                dma((n_sta,)),
-                dma((n_sta,)),
                 dma(()),
+                dma((n_sta // BATCH,)),
+                dma(()),
+                dma((n_sta // BATCH,)),
+                dma(()),
+                dma(()),
+                dma((n_sta // BATCH,)),
+                dma((6,)),
             ],
             compiler_params=pltpu.CompilerParams(collective_id=0, has_side_effects=True),
         )(

time: 43 us -> 30.1 us (0.70)
  Pallas kernels: 41.6 us -> 28.7 us
    pallas_call x1, Pallas kernels: 41.6 us -> 28.7 us  [per_device(): pl.pallas_call(functools.partial(kernel, cfg), out_shape=jax.ShapeDtypeSt...]
where the time goes in v2:
time: 30.1 us; the launch traced here: 30 us
  Pallas kernels  28.7 us (95%)
  local copies, waits for them, and re-layouts  1.28 us (4%)
    pallas_call x1, Pallas kernels, per_device(): pl.pallas_call(functools.partial(kernel, cfg), out_shape=jax.ShapeDtypeSt...  28.7 us
    unnamed x1, local copies, waits for them, and re-layouts  1.28 us

profile of v2, /device:TPU:1, one launch (start us, length us, event | category | flops | bytes accessed | tf_op | source)
XLA Modules:
  0.0 30.0 jit_solution(18269424949164056955)
XLA Ops:
  0.0 28.7 %shard_map.64 = f32[1,1024]{1,0:T(1,128)} custom-call(bf16[48,128]{1,0:T(8,128)(2,1)} %window_hbm.1, bf16[48,599]{1,0:T(8,128)(2,1)} %prior_hbm.1, bf16[32,4,600]{2,1,0:T(4,128)(2,1)} %waves_hbm.1, s32[4,32]{1,0:T(4,128)} %bitcast.3, s32[1,32]{1,0:T(1,128)} %bitcast.5, s32[1,512]{1,0:T(1,128)} %bitcast.4), custom_call_target="tpu_custom_call" | custom-call | tf_op jit(solution)/shard_map/pallas_call | solution.py:395
  28.7 1.3 %copy.8 = f32[1,1024]{1,0:T(1,128)} copy(f32[1,1024]{1,0:T(1,128)} %shard_map.64) | data formatting | bytes 8192

commit v3 on v2

--- a/solution.py
+++ b/solution.py
@@ -84,26 +84,19 @@
     me = lax.axis_index("sta")
     my_t = lax.axis_index("tpl")
 
-    my_y, my_z = me // z_size, me % z_size
     y_size = n_sta // z_size
-
-    def peer_of(k):
-        i, j = k // y_size, k % y_size
-        dz = z_size // 2 + jnp.where(i % 2 == 1, -((i + 1) // 2), i // 2)
-        dy = y_size // 2 + jnp.where(j % 2 == 1, -((j + 1) // 2), j // 2)
-        return ((my_y + dy) % y_size) * z_size + (my_z + dz) % z_size
+    my_y = lax.div(me, z_size)
+    my_z = me - my_y * z_size
+
+    def outward(n):
+        return sorted(range(n), key=lambda d: -min(d, n - d))
+
+    at_z = [lax.rem(my_z + d, z_size) for d in outward(z_size)]
+    at_y = [lax.rem(my_y + d, y_size) * z_size for d in outward(y_size)]
+    peers = [z + y for z in at_z for y in at_y][: n_sta - 1]
+    tpl_peers = [lax.rem(my_t + o, n_tpl) for o in range(1, n_tpl)]
 
     barrier = pltpu.get_barrier_semaphore()
-
-    def greet_sta(k, _):
-        pl.semaphore_signal(barrier, inc=1, device_id={"sta": peer_of(k)}, device_id_type=MESH)
-        return 0
-
-    def greet_tpl(o, _):
-        pl.semaphore_signal(
-            barrier, inc=1, device_id={"tpl": lax.rem(my_t + o, n_tpl)}, device_id_type=MESH
-        )
-        return 0
 
     inputs = [
         pltpu.make_async_copy(src, dst, in_sem.at[n])
@@ -120,8 +113,10 @@
     ]
     for copy in inputs:
         copy.start()
-    lax.fori_loop(0, n_sta - 1, greet_sta, 0)
-    lax.fori_loop(1, n_tpl, greet_tpl, 0)
+    for peer in peers:
+        pl.semaphore_signal(barrier, inc=1, device_id={"sta": peer}, device_id_type=MESH)
+    for peer in tpl_peers:
+        pl.semaphore_signal(barrier, inc=1, device_id={"tpl": peer}, device_id_type=MESH)
     for copy in inputs:
         copy.wait()
 
@@ -198,26 +193,20 @@
         return remote(obuf.at[peer], rres.at[k], res_send, res_recv, {"sta": peer})
 
     def over_tpl(body):
-        def step(o, _):
-            body(lax.rem(my_t + o, n_tpl))
-            return 0
-
-        lax.fori_loop(1, n_tpl, step, 0)
+        for peer in tpl_peers:
+            body(peer)
 
     def over_sta(body):
-        def step(k, _):
-            body(k, peer_of(k))
-            return 0
-
-        lax.fori_loop(0, n_sta - 1, step, 0)
+        for k, peer in enumerate(peers):
+            body(k, peer)
 
     batches = n_sta // BATCH
 
     def batch_of(g):
         return pl.ds(BATCH * g, BATCH - 1 if g == batches - 1 else BATCH)
 
+    over_tpl(lambda peer: win_copy(my_t, peer).start())
     over_sta(lambda k, peer: meta_copy(k, peer).start())
-    over_tpl(lambda peer: win_copy(my_t, peer).start())
     over_sta(lambda k, peer: wave_copy(k, peer).start())
     win[my_t] = window_ref[...]
     rbuf[n_sta - 1] = sbuf[me]
@@ -394,7 +383,7 @@
         dma = pltpu.SemaphoreType.DMA
         return pl.pallas_call(
             functools.partial(kernel, cfg),
-            out_shape=jax.ShapeDtypeStruct((1, lags), F32),
+            out_shape=pltpu.VMEM((1, lags), F32),
             in_specs=[pl.BlockSpec(memory_space=pl.ANY)] * 6,
             out_specs=vmem,
             scratch_shapes=[

time: 30.1 us -> 27.8 us (0.924)
  Pallas kernels: 28.7 us -> 27.1 us
  local copies, waits for them, and re-layouts: 1.28 us -> 0.6 us
    pallas_call x1, Pallas kernels: 28.7 us -> 27.1 us  [per_device(): pl.pallas_call(functools.partial(kernel, cfg), out_shape=pltpu.VMEM((1, l...]
    unnamed x1, local copies, waits for them, and re-layouts: 1.28 us -> 0.6 us
where the time goes in v3:
time: 27.8 us; the launch traced here: 27.7 us
  Pallas kernels  27.1 us (97%)
  local copies, waits for them, and re-layouts  0.6 us (2%)
    pallas_call x1, Pallas kernels, per_device(): pl.pallas_call(functools.partial(kernel, cfg), out_shape=pltpu.VMEM((1, l...  27.1 us
    unnamed x1, local copies, waits for them, and re-layouts  0.6 us

profile of v3, /device:TPU:1, one launch (start us, length us, event | category | flops | bytes accessed | tf_op | source)
XLA Modules:
  0.0 27.7 jit_solution(2902937543642036001)
XLA Ops:
  0.0 27.1 %shard_map.64 = f32[1,1024]{1,0:T(1,128)S(1)} custom-call(bf16[48,128]{1,0:T(8,128)(2,1)} %window_hbm.1, bf16[48,599]{1,0:T(8,128)(2,1)} %prior_hbm.1, bf16[32,4,600]{2,1,0:T(4,128)(2,1)} %waves_hbm.1, s32[4,32]{1,0:T(4,128)} %bitcast.3, s32[1,32]{1,0:T(1,128)} %bitcast.5, s32[1,512]{1,0:T(1,128)} %bitcast.4), custom_call_target="tpu_custom_call" | custom-call | tf_op jit(solution)/shard_map/pallas_call | solution.py:384
  27.1 0.6 %copy.8 = f32[1,1024]{1,0:T(1,128)} copy(f32[1,1024]{1,0:T(1,128)S(1)} %shard_map.64) | data formatting | bytes 8192

commit v4 on v3

--- a/solution.py
+++ b/solution.py
@@ -18,6 +18,7 @@
 LANES = 128
 SUB = 32
 BATCH = 8
+PACK = 16
 QUARTERS = LANES // SUB
 
 
@@ -53,6 +54,8 @@
     flat,
     sbuf,
     rbuf,
+    band,
+    squares,
     mrow,
     mbuf,
     msm,
@@ -98,6 +101,10 @@
 
     barrier = pltpu.get_barrier_semaphore()
 
+    for peer in peers:
+        pl.semaphore_signal(barrier, inc=1, device_id={"sta": peer}, device_id_type=MESH)
+    for peer in tpl_peers:
+        pl.semaphore_signal(barrier, inc=1, device_id={"tpl": peer}, device_id_type=MESH)
     inputs = [
         pltpu.make_async_copy(src, dst, in_sem.at[n])
         for n, (src, dst) in enumerate(
@@ -113,10 +120,6 @@
     ]
     for copy in inputs:
         copy.start()
-    for peer in peers:
-        pl.semaphore_signal(barrier, inc=1, device_id={"sta": peer}, device_id_type=MESH)
-    for peer in tpl_peers:
-        pl.semaphore_signal(barrier, inc=1, device_id={"tpl": peer}, device_id_type=MESH)
     for copy in inputs:
         copy.wait()
 
@@ -164,6 +167,10 @@
     for s in range(n_sta):
         sbuf[s] = normed[cap * s : cap * (s + 1)].astype(BF16)
 
+    e_width = pl.cdiv(length + LANES - 1, LANES) * LANES
+    ahead = iota((e_width, LANES), 0) - iota((e_width, LANES), 1)
+    band[...] = jnp.where((ahead >= 0) & (ahead < length), 1.0, 0.0).astype(BF16)
+
     pl.semaphore_wait(barrier, n_sta + n_tpl - 2)
 
     def remote(src, dst, send, recv, device):
@@ -212,57 +219,6 @@
     rbuf[n_sta - 1] = sbuf[me]
     mbuf[n_sta - 1] = mrow[...]
 
-    over_tpl(lambda peer: win_copy(peer, peer).wait_recv())
-
-    lane_p = iota((8, LANES), 1)
-    prior_tiles = prior_len // LANES
-    prior_rest = prior_len % LANES
-
-    for g in range(rows // 8):
-        r8 = pl.ds(8 * g, 8)
-        old = prior_ref[r8, :].astype(F32)
-        new = jnp.concatenate(
-            [win[p, r8, :].astype(F32) for p in range(n_tpl)] + [jnp.zeros((8, LANES), F32)], axis=1
-        )
-        new = pltpu.roll(new, prior_rest, 1)
-        tail = jnp.concatenate(
-            [old[:, prior_tiles * LANES :], jnp.zeros((8, LANES - prior_rest), F32)], axis=1
-        )
-        joint = jnp.where(lane_p < prior_rest, tail, new[:, :LANES])
-        x = jnp.concatenate([old[:, : prior_tiles * LANES], joint, new[:, LANES:]], axis=1)
-        for b in range(QUARTERS):
-            moved_x = shift_left(x, SUB * b)
-            for m in range(x_blocks):
-                xs[b, pl.ds(pitch * 8 * g + m, 8, stride=pitch), :] = moved_x[
-                    :, LANES * m : LANES * (m + 1)
-                ]
-        sums = {1: x * x}
-        size = 1
-        while 2 * size <= length:
-            sums[2 * size] = sums[size] + shift_left(sums[size], size)
-            size *= 2
-        energy, done = None, 0
-        while size:
-            if length & size:
-                part = shift_left(sums[size], done)
-                energy = part if energy is None else energy + part
-                done += size
-            size //= 2
-        scale = 1.0 / jnp.sqrt(energy[:, :lags] + EPSILON)
-        for a in range(cells):
-            sc[r8, a, :] = scale[:, LANES * a : LANES * (a + 1)]
-
-    def build_row(c, _):
-        for r in range(k_blocks):
-            for b in range(0, QUARTERS, 2):
-                pair = jnp.concatenate(
-                    [xs[b + d, pl.ds(pitch * c + r, cells), :] for d in range(2)], axis=0
-                )
-                xall[c, pl.ds(cells * b, 2 * cells), pl.ds(LANES * r, LANES)] = pair.astype(BF16)
-        return 0
-
-    lax.fori_loop(0, rows, build_row, 0, unroll=4)
-
     quarter = iota((8, LANES), 1) // SUB
 
     def pick(parts):
@@ -271,11 +227,9 @@
             value = jnp.where(quarter == i, parts[i], value)
         return value
 
-    def correlate(s):
+    def shift_waves(s):
         wave = rbuf[s].astype(F32)
-        codes = [msm[s, 0, cap * me + i] for i in range(cap)]
-        local_rows = [code >> (group.bit_length() - 1) for code in codes]
-        shifted = jnp.concatenate(
+        return jnp.concatenate(
             [
                 pltpu.roll(
                     jnp.broadcast_to(wave[i : i + 1], (SUB, k_width)), 0, 1, stride=1, stride_axis=0
@@ -284,6 +238,10 @@
             ],
             axis=0,
         ).astype(BF16)
+
+    def correlate(s, shifted):
+        codes = [msm[s, 0, cap * me + i] for i in range(cap)]
+        local_rows = [code >> (group.bit_length() - 1) for code in codes]
         data = jnp.concatenate([xall[c] for c in local_rows], axis=0)
         found = dot(data, shifted, NT)
         block = lambda i, b: found[SUB * i + cells * b : SUB * i + cells * (b + 1)]
@@ -315,14 +273,66 @@
         here = batch_of(g)
         remote(rbuf.at[here], rbuf.at[here], wave_send, wave_recv.at[g], {"sta": me}).wait_recv()
 
-    meta_here(batches - 1)
+    first = batches - 1
+    meta_here(first)
+    over_tpl(lambda peer: win_copy(peer, peer).wait_recv())
+
+    lane_p = iota((PACK, LANES), 1)
+    prior_tiles = prior_len // LANES
+    prior_rest = prior_len % LANES
+
+    for g in range(rows // PACK):
+        here = pl.ds(PACK * g, PACK)
+        old = prior_ref[here, :].astype(F32)
+        new = jnp.concatenate(
+            [win[p, here, :].astype(F32) for p in range(n_tpl)] + [jnp.zeros((PACK, LANES), F32)],
+            axis=1,
+        )
+        new = pltpu.roll(new, prior_rest, 1)
+        tail = jnp.concatenate(
+            [old[:, prior_tiles * LANES :], jnp.zeros((PACK, LANES - prior_rest), F32)], axis=1
+        )
+        joint = jnp.where(lane_p < prior_rest, tail, new[:, :LANES])
+        x = jnp.concatenate([old[:, : prior_tiles * LANES], joint, new[:, LANES:]], axis=1)
+        for b in range(QUARTERS):
+            moved_x = shift_left(x, SUB * b)
+            for m in range(x_blocks):
+                xs[b, pl.ds(pitch * PACK * g + m, PACK, stride=pitch), :] = moved_x[
+                    :, LANES * m : LANES * (m + 1)
+                ]
+        square = x * x
+        high = square.astype(BF16)
+        squares[here, :] = high
+        squares[pl.ds(rows + PACK * g, PACK), :] = (square - high.astype(F32)).astype(BF16)
+
+    energy = dot(
+        jnp.concatenate([squares[:, pl.ds(LANES * a, e_width)] for a in range(cells)], axis=0),
+        band[...],
+        NN,
+    )
+    for a in range(cells):
+        high_part = energy[2 * rows * a : 2 * rows * a + rows]
+        low_part = energy[2 * rows * a + rows : 2 * rows * (a + 1)]
+        sc[:, a, :] = 1.0 / jnp.sqrt(high_part + low_part + EPSILON)
+
+    def build_row(c, _):
+        for r in range(k_blocks):
+            for b in range(0, QUARTERS, 2):
+                pair = jnp.concatenate(
+                    [xs[b + d, pl.ds(pitch * c + r, cells), :] for d in range(2)], axis=0
+                )
+                xall[c, pl.ds(cells * b, 2 * cells), pl.ds(LANES * r, LANES)] = pair.astype(BF16)
+        return 0
+
+    lax.fori_loop(0, rows, build_row, 0, unroll=4)
+
     for g in reversed(range(batches)):
         if g:
             meta_here(g - 1)
         waves_here(g)
         to_scalars(g).wait()
         for k in range(BATCH):
-            correlate(BATCH * g + k)
+            correlate(BATCH * g + k, shift_waves(BATCH * g + k))
 
     codes = mbuf[...].reshape(n_sta, LANES)
     mine = pltpu.roll(codes, lax.rem(positions - cap * me, positions), 1)
@@ -397,6 +407,8 @@
                 pltpu.VMEM((k_width // LANES, positions, LANES), F32),
                 pltpu.VMEM((n_sta, cap, k_width), BF16),
                 pltpu.VMEM((n_sta, cap, k_width), BF16),
+                pltpu.VMEM((pl.cdiv(length + LANES - 1, LANES) * LANES, LANES), BF16),
+                pltpu.VMEM((2 * rows, pl.cdiv(length - 1 + lags, LANES) * LANES), BF16),
                 pltpu.VMEM((1, positions), I32),
                 pltpu.VMEM((n_sta, 1, positions), I32),
                 pltpu.SMEM((n_sta, 1, positions), I32),

time: 27.8 us -> 26.6 us (0.957)
  the two profiles are of different devices: /device:TPU:1 before, /device:TPU:2 now
where the time goes in v4:
time: 26.6 us; the launch traced here: 26.5 us
  Pallas kernels  25.9 us (97%)
  local copies, waits for them, and re-layouts  0.6 us (2%)
    pallas_call x1, Pallas kernels, per_device(): pl.pallas_call(functools.partial(kernel, cfg), out_shape=pltpu.VMEM((1, l...  25.9 us
    unnamed x1, local copies, waits for them, and re-layouts  0.6 us

profile of v4, /device:TPU:2, one launch (start us, length us, event | category | flops | bytes accessed | tf_op | source)
XLA Modules:
  0.0 26.5 jit_solution(16816879773485515586)
XLA Ops:
  0.0 25.9 %shard_map.64 = f32[1,1024]{1,0:T(1,128)S(1)} custom-call(bf16[48,128]{1,0:T(8,128)(2,1)} %window_hbm.1, bf16[48,599]{1,0:T(8,128)(2,1)} %prior_hbm.1, bf16[32,4,600]{2,1,0:T(4,128)(2,1)} %waves_hbm.1, s32[4,32]{1,0:T(4,128)} %bitcast.3, s32[1,32]{1,0:T(1,128)} %bitcast.5, s32[1,512]{1,0:T(1,128)} %bitcast.4), custom_call_target="tpu_custom_call" | custom-call | tf_op jit(solution)/shard_map/pallas_call | solution.py:394
  25.9 0.6 %copy.8 = f32[1,1024]{1,0:T(1,128)} copy(f32[1,1024]{1,0:T(1,128)S(1)} %shard_map.64) | data formatting | bytes 8192

commit v5 on v4

--- a/solution.py
+++ b/solution.py
@@ -213,8 +213,10 @@
         return pl.ds(BATCH * g, BATCH - 1 if g == batches - 1 else BATCH)
 
     over_tpl(lambda peer: win_copy(my_t, peer).start())
-    over_sta(lambda k, peer: meta_copy(k, peer).start())
-    over_sta(lambda k, peer: wave_copy(k, peer).start())
+    for k, peer in reversed(list(enumerate(peers))):
+        meta_copy(k, peer).start()
+    for k, peer in reversed(list(enumerate(peers))):
+        wave_copy(k, peer).start()
     win[my_t] = window_ref[...]
     rbuf[n_sta - 1] = sbuf[me]
     mbuf[n_sta - 1] = mrow[...]

time: 26.6 us -> 26.5 us (level)
  the two profiles are of different devices: /device:TPU:2 before, /device:TPU:1 now
where the time goes in v5:
time: 26.5 us; the launch traced here: 26 us
  Pallas kernels  25.4 us (96%)
  local copies, waits for them, and re-layouts  0.6 us (2%)
    pallas_call x1, Pallas kernels, per_device(): pl.pallas_call(functools.partial(kernel, cfg), out_shape=pltpu.VMEM((1, l...  25.4 us
    unnamed x1, local copies, waits for them, and re-layouts  0.6 us

profile of v5, /device:TPU:1, one launch (start us, length us, event | category | flops | bytes accessed | tf_op | source)
XLA Modules:
  0.0 26.0 jit_solution(9802801649582412990)
XLA Ops:
  0.0 25.4 %shard_map.64 = f32[1,1024]{1,0:T(1,128)S(1)} custom-call(bf16[48,128]{1,0:T(8,128)(2,1)} %window_hbm.1, bf16[48,599]{1,0:T(8,128)(2,1)} %prior_hbm.1, bf16[32,4,600]{2,1,0:T(4,128)(2,1)} %waves_hbm.1, s32[4,32]{1,0:T(4,128)} %bitcast.3, s32[1,32]{1,0:T(1,128)} %bitcast.5, s32[1,512]{1,0:T(1,128)} %bitcast.4), custom_call_target="tpu_custom_call" | custom-call | tf_op jit(solution)/shard_map/pallas_call | solution.py:396
  25.4 0.6 %copy.8 = f32[1,1024]{1,0:T(1,128)} copy(f32[1,1024]{1,0:T(1,128)S(1)} %shard_map.64) | data formatting | bytes 8192

commit v6 on v5

--- a/solution.py
+++ b/solution.py
@@ -277,35 +277,55 @@
 
     first = batches - 1
     meta_here(first)
-    over_tpl(lambda peer: win_copy(peer, peer).wait_recv())
-
     lane_p = iota((PACK, LANES), 1)
     prior_tiles = prior_len // LANES
     prior_rest = prior_len % LANES
 
+    def square_parts(x):
+        square = x * x
+        high = square.astype(BF16)
+        return high, (square - high.astype(F32)).astype(BF16)
+
+    def keep(g, b, m, value):
+        xs[b, pl.ds(pitch * PACK * g + m, PACK, stride=pitch), :] = value
+
+    old_width = prior_tiles * LANES
     for g in range(rows // PACK):
         here = pl.ds(PACK * g, PACK)
-        old = prior_ref[here, :].astype(F32)
+        old = prior_ref[here, :][:, :old_width].astype(F32)
+        for b in range(QUARTERS):
+            moved_x = shift_left(old, SUB * b)
+            for m in range(prior_tiles if b == 0 else prior_tiles - 1):
+                keep(g, b, m, moved_x[:, LANES * m : LANES * (m + 1)])
+        squares[here, pl.ds(0, old_width)], squares[
+            pl.ds(rows + PACK * g, PACK), pl.ds(0, old_width)
+        ] = square_parts(old)
+
+    over_tpl(lambda peer: win_copy(peer, peer).wait_recv())
+
+    for g in range(rows // PACK):
+        here = pl.ds(PACK * g, PACK)
+        first_tile = prior_tiles - 1
+        old = prior_ref[here, :][:, first_tile * LANES :].astype(F32)
         new = jnp.concatenate(
             [win[p, here, :].astype(F32) for p in range(n_tpl)] + [jnp.zeros((PACK, LANES), F32)],
             axis=1,
         )
         new = pltpu.roll(new, prior_rest, 1)
         tail = jnp.concatenate(
-            [old[:, prior_tiles * LANES :], jnp.zeros((PACK, LANES - prior_rest), F32)], axis=1
+            [old[:, LANES:], jnp.zeros((PACK, LANES - prior_rest), F32)], axis=1
         )
         joint = jnp.where(lane_p < prior_rest, tail, new[:, :LANES])
-        x = jnp.concatenate([old[:, : prior_tiles * LANES], joint, new[:, LANES:]], axis=1)
+        x = jnp.concatenate([old[:, :LANES], joint, new[:, LANES:]], axis=1)
         for b in range(QUARTERS):
             moved_x = shift_left(x, SUB * b)
-            for m in range(x_blocks):
-                xs[b, pl.ds(pitch * PACK * g + m, PACK, stride=pitch), :] = moved_x[
-                    :, LANES * m : LANES * (m + 1)
-                ]
-        square = x * x
-        high = square.astype(BF16)
-        squares[here, :] = high
-        squares[pl.ds(rows + PACK * g, PACK), :] = (square - high.astype(F32)).astype(BF16)
+            for m in range(prior_tiles if b == 0 else first_tile, x_blocks):
+                at = m - first_tile
+                keep(g, b, m, moved_x[:, LANES * at : LANES * (at + 1)])
+        newer = pl.ds(old_width, (x_blocks - prior_tiles) * LANES)
+        squares[here, newer], squares[pl.ds(rows + PACK * g, PACK), newer] = square_parts(
+            x[:, LANES:]
+        )
 
     energy = dot(
         jnp.concatenate([squares[:, pl.ds(LANES * a, e_width)] for a in range(cells)], axis=0),

time: 26.5 us -> 26.5 us (level)
  no operation moved by 1% of the time
where the time goes in v6:
time: 26.5 us; the launch traced here: 26 us
  Pallas kernels  25.4 us (96%)
  local copies, waits for them, and re-layouts  0.6 us (2%)
    pallas_call x1, Pallas kernels, per_device(): pl.pallas_call(functools.partial(kernel, cfg), out_shape=pltpu.VMEM((1, l...  25.4 us
    unnamed x1, local copies, waits for them, and re-layouts  0.6 us

profile of v6, /device:TPU:1, one launch (start us, length us, event | category | flops | bytes accessed | tf_op | source)
XLA Modules:
  0.0 26.0 jit_solution(11341792003154864135)
XLA Ops:
  0.0 25.4 %shard_map.64 = f32[1,1024]{1,0:T(1,128)S(1)} custom-call(bf16[48,128]{1,0:T(8,128)(2,1)} %window_hbm.1, bf16[48,599]{1,0:T(8,128)(2,1)} %prior_hbm.1, bf16[32,4,600]{2,1,0:T(4,128)(2,1)} %waves_hbm.1, s32[4,32]{1,0:T(4,128)} %bitcast.3, s32[1,32]{1,0:T(1,128)} %bitcast.5, s32[1,512]{1,0:T(1,128)} %bitcast.4), custom_call_target="tpu_custom_call" | custom-call | tf_op jit(solution)/shard_map/pallas_call | solution.py:416
  25.4 0.6 %copy.8 = f32[1,1024]{1,0:T(1,128)} copy(f32[1,1024]{1,0:T(1,128)S(1)} %shard_map.64) | data formatting | bytes 8192
